TPU v7x, 32 devices: a whole 2x2x4 slice. The times are simulated.
32 devices in a mesh: rep: 8 (over z, core), shard: 4 (over y, x).
Axes of the slice: x: 2, y: 2, z: 4, core: 2. Of those that a mesh axis runs over, the one named last changes fastest.
Arguments:
- tokens: bfloat16 [4096, 1536], P(('rep', 'shard')), may hold values from -6 to 6
- cotangent: bfloat16 [4096, 1536], P(('rep', 'shard')), may hold values from -6 to 6
- lengths: int32 [8], P('rep'), may hold values from 128 to 512, as said below
- gain_one: bfloat16 [1536], P('shard'), may hold values from 0.5 to 1.5
- w_query: bfloat16 [1536, 1536], P('shard'), may hold values from -0.15625 to 0.15625
- w_key: bfloat16 [1536, 1536], P('shard'), may hold values from -0.15625 to 0.15625
- w_value: bfloat16 [1536, 1536], P('shard'), may hold values from -0.15625 to 0.15625
- w_path: bfloat16 [1536, 1536], P('shard'), may hold values from -0.15625 to 0.15625
- w_beta: bfloat16 [1536, 12], P('shard'), may hold values from -0.15625 to 0.15625
- w_out: bfloat16 [1536, 1536], P('shard'), may hold values from -0.625 to 0.625
- gain_two: bfloat16 [1536], P('shard'), may hold values from 0.5 to 1.5
- w_gate: bfloat16 [1536, 4096], P('shard'), may hold values from -0.15625 to 0.15625
- w_up: bfloat16 [1536, 4096], P('shard'), may hold values from -0.15625 to 0.15625
- w_down: bfloat16 [4096, 1536], P('shard'), may hold values from -0.09375 to 0.09375
Outputs:
- output: bfloat16 [4096, 1536], P(('rep', 'shard'))
- input_grad: bfloat16 [4096, 1536], P(('rep', 'shard'))
- grad_gain_one: float32 [1536], P('shard')
- grad_w_query: float32 [1536, 1536], P('shard')
- grad_w_key: float32 [1536, 1536], P('shard')
- grad_w_value: float32 [1536, 1536], P('shard')
- grad_w_path: float32 [1536, 1536], P('shard')
- grad_w_beta: float32 [1536, 12], P('shard')
- grad_w_out: float32 [1536, 1536], P('shard')
- grad_gain_two: float32 [1536], P('shard')
- grad_w_gate: float32 [1536, 4096], P('shard')
- grad_w_up: float32 [1536, 4096], P('shard')
- grad_w_down: float32 [4096, 1536], P('shard')
- rms_input: float32 [], replicated
- rms_attn: float32 [], replicated
- rms_feed: float32 [], replicated
Inputs may be any that keep to these rules, and one draw needn't show every extreme that they name: Sequence r fills the first lengths[r] of its 512 slots; at least one sequence fills all of them.
All inputs are finite; a program needn't handle non-finite values.
Results may differ from a plain program's by a relative error of at most 0.02.
Values may be sent and summed in bfloat16 or wider, within the bound.
No kernel may reach another device: no remote copies, remote signals or barrier semaphores. Data moves between devices by JAX's collectives and lax.ppermute only.
A program may use at most 320 MiB of HBM per device.

v0:
```python
import jax
import jax.numpy as jnp
from jax import lax
from jax.sharding import PartitionSpec as P

eps = 1e-06
highest = lax.Precision.HIGHEST


def rms_norm(value, gain_vec):
    factor = lax.rsqrt(jnp.mean(value * value, axis=-1, keepdims=True) + eps)
    return value * factor * gain_vec


def unit_rows(raw):
    return raw * lax.rsqrt(jnp.sum(raw * raw, axis=-1, keepdims=True) + eps)


def rounded(value):
    return lax.optimization_barrier(value.astype(jnp.bfloat16)).astype(jnp.float32)


def round_pass(value):
    return value + lax.stop_gradient(rounded(value) - value)


def split_heads(matrix, head_count):
    return matrix.reshape(matrix.shape[0], head_count, -1).transpose(1, 0, 2)


def join_heads(matrix):
    return matrix.transpose(1, 0, 2).reshape(matrix.shape[1], -1)


def mul_low(left, right):
    return jnp.dot(left, right, preferred_element_type=jnp.float32)


def back_mul(grad_rows, weight):
    return jnp.einsum("tg,fg->tf", grad_rows, weight, preferred_element_type=jnp.float32)


def weight_grad(left, right):
    return jnp.einsum("tf,tg->fg", left, right, preferred_element_type=jnp.float32)


def masks(block_len):
    row_ids = jnp.arange(block_len)[:, None]
    col_ids = jnp.arange(block_len)[None, :]
    return (col_ids < row_ids, col_ids <= row_ids)


def block_system(direction, beta_rate):
    block_len = direction.shape[1]
    strictly, up_to = masks(block_len)
    gram = jnp.einsum("htd,hsd->hts", direction, direction, precision=highest)
    return jnp.eye(block_len, dtype=jnp.float32)[None] + jnp.where(
        strictly[None], gram * beta_rate[:, None, :], 0.0
    )


def own_context(keyset, values, direction, beta_rate):
    system = block_system(direction, beta_rate)
    strictly, up_to = masks(keyset.shape[1])
    coupled = jnp.where(
        strictly[None], jnp.einsum("htd,hjd->htj", direction, keyset, precision=highest), 0.0
    )
    solved = jax.scipy.linalg.solve_triangular(system, coupled, lower=True, unit_diagonal=True)
    scaled_dir = direction * beta_rate[:, :, None]
    key_end = keyset - jnp.einsum("htj,htd->hjd", solved, scaled_dir, precision=highest)
    through = jax.scipy.linalg.solve_triangular(system, direction, lower=True, unit_diagonal=True)
    block_map = jnp.eye(direction.shape[2], dtype=jnp.float32)[None] - jnp.einsum(
        "htm,htn->hmn", scaled_dir, through, precision=highest
    )
    return (join_heads(key_end), join_heads(values), block_map[None])


def attend(
    queries, keyset, values, direction, beta_rate, key_far, value_far, maps_far, my_block, length
):
    head_count, block_len, head_width = queries.shape
    blocks = maps_far.shape[0]
    score_scale = head_width ** (-0.5)
    strictly, up_to = masks(block_len)
    system = block_system(direction, beta_rate)
    coupled = jnp.where(
        strictly[None], jnp.einsum("htd,hjd->htj", direction, keyset, precision=highest), 0.0
    )
    solved = jax.scipy.linalg.solve_triangular(system, coupled, lower=True, unit_diagonal=True)
    crossing = (
        jnp.where(
            up_to[None], jnp.einsum("hid,htd->hit", queries, direction, precision=highest), 0.0
        )
        * beta_rate[:, None, :]
    )
    near_scores = (
        jnp.einsum("hid,hjd->hij", queries, keyset, precision=highest)
        - jnp.einsum("hit,htj->hij", crossing, solved, precision=highest)
    ) * score_scale
    back_solved = jax.scipy.linalg.solve_triangular(
        system, crossing.transpose(0, 2, 1), lower=True, trans=1, unit_diagonal=True
    )
    moved = queries - jnp.einsum("hti,htd->hid", back_solved, direction, precision=highest)

    def advance(carried, item_pair):
        block_map, index = item_pair
        updated = jnp.einsum("hid,hde->hie", carried, block_map, precision=highest)
        return (jnp.where(index < my_block, updated, carried), carried)

    unused, reached = lax.scan(advance, moved, (maps_far, jnp.arange(blocks)), reverse=True)
    far_keys = key_far.reshape(blocks, block_len, head_count, head_width)
    far_values = value_far.reshape(blocks, block_len, head_count, head_width)
    far_scores = jnp.einsum("ehid,ejhd->ehij", reached, far_keys, precision=highest) * score_scale
    positions = jnp.arange(block_len)
    near_ok = up_to[None] & ((my_block * block_len + positions)[None, None, :] < length)
    block_ids = jnp.arange(blocks)
    far_ok = (block_ids[:, None, None, None] < my_block) & (
        (block_ids[:, None] * block_len + positions[None, :])[:, None, None, :] < length
    )
    near_masked = jnp.where(near_ok, near_scores, -1e30)
    far_masked = jnp.where(far_ok, far_scores, -1e30)
    row_max = jnp.maximum(jnp.max(near_masked, axis=2), jnp.max(far_masked, axis=(0, 3)))[
        :, :, None
    ]
    row_total = jnp.sum(jnp.where(near_ok, jnp.exp(near_masked - row_max), 0.0), axis=2) + jnp.sum(
        jnp.where(far_ok, jnp.exp(far_masked - row_max[None]), 0.0), axis=(0, 3)
    )
    log_total = row_max + jnp.log(row_total)[:, :, None]
    near_probs = round_pass(jnp.where(near_ok, jnp.exp(near_masked - log_total), 0.0))
    far_probs = round_pass(jnp.where(far_ok, jnp.exp(far_masked - log_total[None]), 0.0))
    return jnp.einsum("hij,hjd->hid", near_probs, values, precision=highest) + jnp.einsum(
        "ehij,ejhd->hid", far_probs, far_values, precision=highest
    )


def per_device(
    tokens,
    cotangent,
    lengths,
    gain_one,
    w_query,
    w_key,
    w_value,
    w_path,
    w_beta,
    w_out,
    gain_two,
    w_gate,
    w_up,
    w_down,
):
    gain_a, query_w, key_w, value_w, path_w, beta_w, out_w, gain_b, gate_w, up_w, down_w = (
        lax.all_gather(gain_one, "shard", axis=0, tiled=True),
        lax.all_gather(w_query, "shard", axis=0, tiled=True),
        lax.all_gather(w_key, "shard", axis=0, tiled=True),
        lax.all_gather(w_value, "shard", axis=0, tiled=True),
        lax.all_gather(w_path, "shard", axis=0, tiled=True),
        lax.all_gather(w_beta, "shard", axis=0, tiled=True),
        lax.all_gather(w_out, "shard", axis=0, tiled=True),
        lax.all_gather(gain_two, "shard", axis=0, tiled=True),
        lax.all_gather(w_gate, "shard", axis=0, tiled=True),
        lax.all_gather(w_up, "shard", axis=0, tiled=True),
        lax.all_gather(w_down, "shard", axis=0, tiled=True),
    )
    block_len = tokens.shape[0]
    width = tokens.shape[1]
    head_count = beta_w.shape[1]
    my_block = lax.axis_index("shard")
    length = lengths[0]
    live_mask = (my_block * block_len + jnp.arange(block_len) < length).astype(jnp.float32)[:, None]
    stream_in = tokens.astype(jnp.float32)
    normed_f, norm_pull = jax.vjp(rms_norm, stream_in, gain_a.astype(jnp.float32))
    normed = normed_f.astype(jnp.bfloat16)
    queries = split_heads(rounded(mul_low(normed, query_w)), head_count)
    keyset = split_heads(rounded(mul_low(normed, key_w)), head_count)
    values_h = split_heads(rounded(mul_low(normed, value_w)), head_count)
    raw = mul_low(normed, path_w).reshape(block_len, head_count, -1)
    direction_f, unit_pull = jax.vjp(unit_rows, raw)
    direction = rounded(direction_f).transpose(1, 0, 2)
    beta_rate = 2.0 * jax.nn.sigmoid(mul_low(normed, beta_w))
    (key_end, value_own, map_own), context_pull = jax.vjp(
        own_context, keyset, values_h, direction, beta_rate.T
    )
    key_far, value_far, maps_far = (
        lax.all_gather(key_end.astype(jnp.bfloat16), "shard", axis=0, tiled=True).astype(
            key_end.dtype
        ),
        lax.all_gather(value_own.astype(jnp.bfloat16), "shard", axis=0, tiled=True).astype(
            value_own.dtype
        ),
        lax.all_gather(map_own.astype(jnp.bfloat16), "shard", axis=0, tiled=True).astype(
            map_own.dtype
        ),
    )

    def local_attend(
        queries, keyset, values_h, direction, beta_heads, key_far, value_far, maps_far
    ):
        return attend(
            queries,
            keyset,
            values_h,
            direction,
            beta_heads,
            key_far,
            value_far,
            maps_far,
            my_block,
            length,
        )

    heads_out, attend_pull = jax.vjp(
        local_attend,
        queries,
        keyset,
        values_h,
        direction,
        beta_rate.T,
        key_far,
        value_far,
        maps_far,
    )
    mixed = join_heads(heads_out).astype(jnp.bfloat16)
    attn_out = mul_low(mixed, out_w)
    stream = stream_in + live_mask * attn_out
    normed_two_f, norm_two_pull = jax.vjp(rms_norm, stream, gain_b.astype(jnp.float32))
    normed_two = normed_two_f.astype(jnp.bfloat16)
    gate_pre = mul_low(normed_two, gate_w)
    up_pre = mul_low(normed_two, up_w)
    gate_sig = jax.nn.sigmoid(gate_pre)
    hidden = (gate_pre * gate_sig * up_pre).astype(jnp.bfloat16)
    feed_out = mul_low(hidden, down_w)
    output = (live_mask * (stream + feed_out)).astype(jnp.bfloat16)
    cot_rows = cotangent.astype(jnp.float32) * live_mask
    d_feed = cot_rows.astype(jnp.bfloat16)
    d_hidden = back_mul(d_feed, down_w)
    d_gate = (d_hidden * up_pre * gate_sig * (1.0 + gate_pre * (1.0 - gate_sig))).astype(
        jnp.bfloat16
    )
    d_up = (d_hidden * gate_pre * gate_sig).astype(jnp.bfloat16)
    d_normed_two = back_mul(d_gate, gate_w) + back_mul(d_up, up_w)
    d_stream_norm, grad_gain_b = norm_two_pull(d_normed_two)
    d_stream = cot_rows + d_stream_norm
    d_attn = (live_mask * d_stream).astype(jnp.bfloat16)
    d_mixed = split_heads(rounded(back_mul(d_attn, out_w)), head_count)
    (
        d_queries,
        d_keys_near,
        d_values_near,
        d_dir_near,
        d_beta_near,
        d_key_far,
        d_value_far,
        d_maps_far,
    ) = attend_pull(d_mixed)
    d_key_end, d_value_own, d_map_own = (
        lax.psum_scatter(
            d_key_far.astype(jnp.bfloat16), "shard", scatter_dimension=0, tiled=True
        ).astype(jnp.float32),
        lax.psum_scatter(
            d_value_far.astype(jnp.bfloat16), "shard", scatter_dimension=0, tiled=True
        ).astype(jnp.float32),
        lax.psum_scatter(
            d_maps_far.astype(jnp.bfloat16), "shard", scatter_dimension=0, tiled=True
        ).astype(jnp.float32),
    )
    d_keys_ctx, d_values_ctx, d_dir_ctx, d_beta_ctx = context_pull(
        (d_key_end, d_value_own, d_map_own)
    )
    d_query_b = join_heads(d_queries).astype(jnp.bfloat16)
    d_key_b = join_heads(d_keys_near + d_keys_ctx).astype(jnp.bfloat16)
    d_value_b = join_heads(d_values_near + d_values_ctx).astype(jnp.bfloat16)
    (d_raw,) = unit_pull((d_dir_near + d_dir_ctx).transpose(1, 0, 2))
    d_raw_b = d_raw.reshape(block_len, -1).astype(jnp.bfloat16)
    d_beta_total = (d_beta_near + d_beta_ctx).T
    d_logit_b = (d_beta_total * beta_rate * (1.0 - 0.5 * beta_rate)).astype(jnp.bfloat16)
    d_normed = (
        back_mul(d_query_b, query_w)
        + back_mul(d_key_b, key_w)
        + back_mul(d_value_b, value_w)
        + back_mul(d_raw_b, path_w)
        + back_mul(d_logit_b, beta_w)
    )
    d_stream_in, grad_gain_a = norm_pull(d_normed)
    input_grad = (d_stream_in + d_stream).astype(jnp.bfloat16)
    g_query = weight_grad(normed, d_query_b)
    g_key = weight_grad(normed, d_key_b)
    g_value = weight_grad(normed, d_value_b)
    g_path = weight_grad(normed, d_raw_b)
    g_beta = weight_grad(normed, d_logit_b)
    g_out = weight_grad(mixed, d_attn)
    g_gate = weight_grad(normed_two, d_gate)
    g_up = weight_grad(normed_two, d_up)
    g_down = weight_grad(hidden, d_feed)
    part_sums = (
        lax.psum_scatter(
            grad_gain_a.astype(jnp.bfloat16), "shard", scatter_dimension=0, tiled=True
        ).astype(jnp.float32),
        lax.psum_scatter(
            g_query.astype(jnp.bfloat16), "shard", scatter_dimension=0, tiled=True
        ).astype(jnp.float32),
        lax.psum_scatter(
            g_key.astype(jnp.bfloat16), "shard", scatter_dimension=0, tiled=True
        ).astype(jnp.float32),
        lax.psum_scatter(
            g_value.astype(jnp.bfloat16), "shard", scatter_dimension=0, tiled=True
        ).astype(jnp.float32),
        lax.psum_scatter(
            g_path.astype(jnp.bfloat16), "shard", scatter_dimension=0, tiled=True
        ).astype(jnp.float32),
        lax.psum_scatter(
            g_beta.astype(jnp.bfloat16), "shard", scatter_dimension=0, tiled=True
        ).astype(jnp.float32),
        lax.psum_scatter(
            g_out.astype(jnp.bfloat16), "shard", scatter_dimension=0, tiled=True
        ).astype(jnp.float32),
        lax.psum_scatter(
            grad_gain_b.astype(jnp.bfloat16), "shard", scatter_dimension=0, tiled=True
        ).astype(jnp.float32),
        lax.psum_scatter(
            g_gate.astype(jnp.bfloat16), "shard", scatter_dimension=0, tiled=True
        ).astype(jnp.float32),
        lax.psum_scatter(
            g_up.astype(jnp.bfloat16), "shard", scatter_dimension=0, tiled=True
        ).astype(jnp.float32),
        lax.psum_scatter(
            g_down.astype(jnp.bfloat16), "shard", scatter_dimension=0, tiled=True
        ).astype(jnp.float32),
    )
    owned = (
        lax.psum(part_sums[0].astype(jnp.bfloat16), "rep").astype(jnp.float32),
        lax.psum(part_sums[1].astype(jnp.bfloat16), "rep").astype(jnp.float32),
        lax.psum(part_sums[2].astype(jnp.bfloat16), "rep").astype(jnp.float32),
        lax.psum(part_sums[3].astype(jnp.bfloat16), "rep").astype(jnp.float32),
        lax.psum(part_sums[4].astype(jnp.bfloat16), "rep").astype(jnp.float32),
        lax.psum(part_sums[5].astype(jnp.bfloat16), "rep").astype(jnp.float32),
        lax.psum(part_sums[6].astype(jnp.bfloat16), "rep").astype(jnp.float32),
        lax.psum(part_sums[7].astype(jnp.bfloat16), "rep").astype(jnp.float32),
        lax.psum(part_sums[8].astype(jnp.bfloat16), "rep").astype(jnp.float32),
        lax.psum(part_sums[9].astype(jnp.bfloat16), "rep").astype(jnp.float32),
        lax.psum(part_sums[10].astype(jnp.bfloat16), "rep").astype(jnp.float32),
    )
    sq_input, sq_attn, sq_feed, live_total = lax.psum(
        (
            jnp.sum(live_mask * stream_in * stream_in),
            jnp.sum(live_mask * attn_out * attn_out),
            jnp.sum(live_mask * feed_out * feed_out),
            jnp.sum(live_mask),
        ),
        ("rep", "shard"),
    )
    denom = live_total * width
    return (
        output,
        input_grad,
        owned[0],
        owned[1],
        owned[2],
        owned[3],
        owned[4],
        owned[5],
        owned[6],
        owned[7],
        owned[8],
        owned[9],
        owned[10],
        jnp.sqrt(sq_input / denom),
        jnp.sqrt(sq_attn / denom),
        jnp.sqrt(sq_feed / denom),
    )


def solution(mesh):
    return jax.shard_map(
        per_device,
        mesh=mesh,
        in_specs=(
            P(("rep", "shard"), None),
            P(("rep", "shard"), None),
            P("rep"),
            P("shard"),
            P("shard", None),
            P("shard", None),
            P("shard", None),
            P("shard", None),
            P("shard", None),
            P("shard", None),
            P("shard"),
            P("shard", None),
            P("shard", None),
            P("shard", None),
        ),
        out_specs=(
            P(("rep", "shard"), None),
            P(("rep", "shard"), None),
            P("shard"),
            P("shard", None),
            P("shard", None),
            P("shard", None),
            P("shard", None),
            P("shard", None),
            P("shard", None),
            P("shard"),
            P("shard", None),
            P("shard", None),
            P("shard", None),
            P(),
            P(),
            P(),
        ),
        check_vma=False,
    )
```

profile of v0, /device:TPU:0, one launch (start us, length us, event | category | flops | bytes accessed | tf_op | source)
XLA Modules:
  0.0 1988.5 jit_solution(15971856994298718647)
XLA Ops:
  29.4 40.5 %all-gather.19.cloned.1.call-done = bf16[1536,1536]{1,0:T(8,128)(2,1)} async-done(((bf16[384,1536]{1,0:T(8,128)(2,1)}), bf16[1536,1536]{1,0:T(8,128)(2,1)}) %all-gather.19.cloned.1.call-update) | async-done | bytes 4718608 | tf_op jit(solution)/shard_map/all_gather | solution.py:157
  76.4 117.9 %custom-call.16 = f32[12,1,128,128]{2,3,1,0:T(8,128)S(1)} custom-call(f32[12,1,128,128]{3,2,1,0:T(8,128)S(1)} %add_bitcast_fusion), custom_call_target="InvertDiagBlocksLowerTriangular" | custom-call | tf_op jit(solution)/shard_map/jvp(jit(_solve_triangular))/vmap()/triangular_solve/custom-call.1 | solution.py:89
  228.1 20.2 %all-gather.15.cloned.1.call-done = bf16[1536,1536]{1,0:T(8,128)(2,1)} async-done(((bf16[384,1536]{1,0:T(8,128)(2,1)}), bf16[1536,1536]{1,0:T(8,128)(2,1)}) %all-gather.15.cloned.1.call-update) | async-done | bytes 4718608 | tf_op jit(solution)/shard_map/all_gather | solution.py:154
  263.0 18.5 all-gather.35.cloned.1.call-done
  285.0 29.7 %all-gather.21.cloned.1.call-done = bf16[512,1536]{0,1:T(8,128)(2,1)} async-done(((bf16[128,1536]{0,1:T(8,128)(2,1)}), bf16[512,1536]{0,1:T(8,128)(2,1)}) %all-gather.21.cloned.1.call-update) | async-done | bytes 1572880 | tf_op jit(solution)/shard_map/all_gather | solution.py:185
  321.8 19.7 while.31
  371.0 36.0 %all-gather.27.cloned.1.call-done = bf16[1536,1536]{1,0:T(8,128)(2,1)} async-done(((bf16[384,1536]{1,0:T(8,128)(2,1)}), bf16[1536,1536]{1,0:T(8,128)(2,1)}) %all-gather.27.cloned.1.call-update) | async-done | bytes 4718608 | tf_op jit(solution)/shard_map/all_gather | solution.py:159
  413.2 118.2 %all-gather.29.cloned.1.call-done = bf16[1536,4096]{1,0:T(8,128)(2,1)} async-done(((bf16[384,4096]{1,0:T(8,128)(2,1)}), bf16[1536,4096]{1,0:T(8,128)(2,1)}) %all-gather.29.cloned.1.call-update) | async-done | bytes 12582928 | tf_op jit(solution)/shard_map/all_gather | solution.py:161
  539.3 116.4 %all-gather.31.cloned.1.call-done = bf16[1536,4096]{1,0:T(8,128)(2,1)} async-done(((bf16[384,4096]{1,0:T(8,128)(2,1)}), bf16[1536,4096]{1,0:T(8,128)(2,1)}) %all-gather.31.cloned.1.call-update) | async-done | bytes 12582928 | tf_op jit(solution)/shard_map/all_gather | solution.py:162
  663.5 116.5 %all-gather.33.cloned.1.call-done = bf16[4096,1536]{1,0:T(8,128)(2,1)} async-done(((bf16[1024,1536]{1,0:T(8,128)(2,1)}), bf16[4096,1536]{1,0:T(8,128)(2,1)}) %all-gather.33.cloned.1.call-update) | async-done | bytes 12582928 | tf_op jit(solution)/shard_map/all_gather | solution.py:163
  780.1 10.2 multiply_convert_fusion
  790.4 10.2 fusion.205
  864.6 41.8 %while.32 = (s32[]{:T(128)}, f32[12,128,128]{2,1,0:T(8,128)}, bf16[4,12,128,128]{3,2,1,0:T(8,128)(2,1)}, f32[4,12,128,128]{3,2,1,0:T(8,128)}, pred[4]{0:T(512)(1...) while((s32[]{:T(128)}, f32[12,128,128]{2,1,0:T(8,128)}, ...), condition=%wide.region_16.19_spmd.clone, body=%wide.region_15.18_spmd.clone.sunk | while | flops 605552640 | bytes 7869556 | solution.py:110
  1022.4 41.7 %reduce-scatter.29.cloned.1.call-done = bf16[384,1536]{1,0:T(8,128)(2,1)} async-done(((bf16[1536,1536]{1,0:T(8,128)(2,1)}), bf16[384,1536]{1,0:T(8,128)(2,1)}) %reduce-scatter.29.cloned.1.call-update) | async-done | bytes 1179664 | tf_op jit(solution)/shard_map/reduce_scatter | solution.py:314
  1064.0 60.5 %reduce-scatter.23.cloned.1.call-done = bf16[384,1536]{1,0:T(8,128)(2,1)} async-done(((bf16[1536,1536]{1,0:T(8,128)(2,1)}), bf16[384,1536]{1,0:T(8,128)(2,1)}) %reduce-scatter.23.cloned.1.call-update) | async-done | bytes 1179664 | tf_op jit(solution)/shard_map/reduce_scatter | solution.py:302
  1124.6 60.6 %reduce-scatter.25.cloned.1.call-done = bf16[384,1536]{1,0:T(8,128)(2,1)} async-done(((bf16[1536,1536]{1,0:T(8,128)(2,1)}), bf16[384,1536]{1,0:T(8,128)(2,1)}) %reduce-scatter.25.cloned.1.call-update) | async-done | bytes 1179664 | tf_op jit(solution)/shard_map/reduce_scatter | solution.py:305
  1185.1 60.1 %reduce-scatter.27.cloned.1.call-done = bf16[384,1536]{1,0:T(8,128)(2,1)} async-done(((bf16[1536,1536]{1,0:T(8,128)(2,1)}), bf16[384,1536]{1,0:T(8,128)(2,1)}) %reduce-scatter.27.cloned.1.call-update) | async-done | bytes 1179664 | tf_op jit(solution)/shard_map/reduce_scatter | solution.py:308
  1245.2 123.7 %reduce-scatter.31.cloned.1.call-done = bf16[384,4096]{1,0:T(8,128)(2,1)} async-done(((bf16[1536,4096]{1,0:T(8,128)(2,1)}), bf16[384,4096]{1,0:T(8,128)(2,1)}) %reduce-scatter.31.cloned.1.call-update) | async-done | bytes 3145744 | tf_op jit(solution)/shard_map/reduce_scatter | solution.py:320
  1368.9 123.9 %reduce-scatter.33.cloned.1.call-done = bf16[384,4096]{1,0:T(8,128)(2,1)} async-done(((bf16[1536,4096]{1,0:T(8,128)(2,1)}), bf16[384,4096]{1,0:T(8,128)(2,1)}) %reduce-scatter.33.cloned.1.call-update) | async-done | bytes 3145744 | tf_op jit(solution)/shard_map/reduce_scatter | solution.py:323
  1492.8 123.9 %reduce-scatter.35.cloned.1.call-done = bf16[1024,1536]{1,0:T(8,128)(2,1)} async-done(((bf16[4096,1536]{1,0:T(8,128)(2,1)}), bf16[1024,1536]{1,0:T(8,128)(2,1)}) %reduce-scatter.35.cloned.1.call-update) | async-done | bytes 3145744 | tf_op jit(solution)/shard_map/reduce_scatter | solution.py:326
  1633.7 40.3 %all-reduce.3 = (f32[]{:T(128)}, f32[]{:T(128)}, f32[]{:T(128)}, f32[]{:T(128)}) all-reduce(f32[]{:T(128)} %get-tuple-element.278, f32[]{:T(128)} %get-tuple-element.326, f32[]{:T(128)} %get-tuple-element.280, f32[]{:T(128)} %get-tuple-element.279), channel_id=1, replica_groups=mesh['rep'=8,'shard'=4] {'rep','shard'}, use_global_device_ids=true, to_apply=%region_52.55 | all-reduce | flops 4 | bytes 32 | tf_op jit(solution)/shard_map/psum | solution.py:343
  1674.0 10.8 all-reduce.6
  1689.7 28.2 %all-reduce.4 = (bf16[384]{0:T(512)(128)(2,1)S(1)}, bf16[384,12]{0,1:T(8,128)(2,1)S(1)}, bf16[384]{0:T(512)(128)(2,1)S(1)}) all-reduce(bf16[384]{0:T(512)(128)(2,1)S(1)} %dynamic-slice.3, bf16[384,12]{0,1:T(8,128)(2,1)S(1)} %copy.335, bf16[384]{0:T(512)(128)(2,1)S(1)} %dynamic-slice.5), channel_id=1, replica_groups=mesh['rep'=8,'shard'=4] {'rep'}, use_global_device_ids=true, to_apply=%region_29.32 | all-reduce | flops 5376 | bytes 21504 | tf_op jit(solution)/shard_map/psum | solution.py:331
  1719.6 238.0 %all-reduce.9.cloned.1.call-done = (bf16[384,1536]{1,0:T(8,128)(2,1)}, bf16[384,1536]{1,0:T(8,128)(2,1)}, bf16[384,1536]{1,0:T(8,128)(2,1)}, bf16[384,1536]{1,0:...) async-done(((bf16[384,1536]{1,0:T(8,128)(2,1)}, bf16[384,1536]{1,0:T(8,128)(2,1)}, ...) | async-done | bytes 15335440 | tf_op jit(solution)/shard_map/psum | solution.py:332
  (553 shorter events, 415.9 us)
Async XLA Ops:
  7.2 62.7 %all-gather.19.cloned.1.call-start = ((), (), s32[]{:S(2)}) async-start(), calls=%async_computation.14 | async-start | bytes 5898240 | tf_op jit(solution)/shard_map/all_gather | solution.py:157
  7.9 191.4 %all-gather.17.cloned.1.call-start = ((), (), s32[]{:S(2)}) async-start(), calls=%async_computation.13 | async-start | bytes 5898240 | tf_op jit(solution)/shard_map/all_gather | solution.py:155
  8.7 198.7 %all-gather.23.cloned.1.call-start = ((), (), s32[]{:S(2)}) async-start(), calls=%async_computation.16 | async-start | bytes 5898240 | tf_op jit(solution)/shard_map/all_gather | solution.py:156
  9.4 238.9 %all-gather.15.cloned.1.call-start = ((), (), s32[]{:S(2)}) async-start(), calls=%async_computation.12 | async-start | bytes 5898240 | tf_op jit(solution)/shard_map/all_gather | solution.py:154
  10.0 271.5 %all-gather.35.cloned.1.call-start = ((), (), s32[]{:S(2)}) async-start(), calls=%async_computation.30 | async-start | bytes 1966080 | tf_op jit(solution)/shard_map/all_gather | solution.py:191
  199.0 115.6 %all-gather.21.cloned.1.call-start = ((), (), s32[]{:S(2)}) async-start(), calls=%async_computation.15 | async-start | bytes 1966080 | tf_op jit(solution)/shard_map/all_gather | solution.py:185
  207.4 143.5 %all-gather.25.cloned.1.call-start = ((), (), s32[]{:S(2)}) async-start(), calls=%async_computation.17 | async-start | bytes 1966080 | tf_op jit(solution)/shard_map/all_gather | solution.py:188
  211.4 195.7 %all-gather.27.cloned.1.call-start = ((), (), s32[]{:S(2)}) async-start(), calls=%async_computation.18 | async-start | bytes 5898240 | tf_op jit(solution)/shard_map/all_gather | solution.py:159
  212.1 319.3 %all-gather.29.cloned.1.call-start = ((), (), s32[]{:S(2)}) async-start(), calls=%async_computation.19 | async-start | bytes 15728640 | tf_op jit(solution)/shard_map/all_gather | solution.py:161
  212.9 442.8 %all-gather.31.cloned.1.call-start = ((), (), s32[]{:S(2)}) async-start(), calls=%async_computation.20 | async-start | bytes 15728640 | tf_op jit(solution)/shard_map/all_gather | solution.py:162
  213.5 566.6 %all-gather.33.cloned.1.call-start = ((), (), s32[]{:S(2)}) async-start(), calls=%async_computation.21 | async-start | bytes 15728640 | tf_op jit(solution)/shard_map/all_gather | solution.py:163
  214.2 724.2 %reduce-scatter.37.cloned.1.call-start = ((), (), s32[]{:S(2)}) async-start(), calls=%async_computation.31 | async-start | bytes 1966080
  843.5 108.3 %reduce-scatter.39.cloned.1.call-start = ((), (), s32[]{:S(2)}) async-start(), calls=%async_computation.32 | async-start | bytes 1966080
  856.0 116.3 %reduce-scatter.43.cloned.1.call-start = ((), (), s32[]{:S(2)}) async-start(), calls=%async_computation.34 | async-start | bytes 1966080
  906.5 115.9 %reduce-scatter.21.cloned.1.call-start = ((), (), s32[]{:S(2)}) async-start(), calls=%async_computation.22 | async-start | bytes 5898240 | tf_op jit(solution)/shard_map/reduce_scatter | solution.py:299
  923.5 140.5 %reduce-scatter.29.cloned.1.call-start = ((), (), s32[]{:S(2)}) async-start(), calls=%async_computation.26 | async-start | bytes 5898240 | tf_op jit(solution)/shard_map/reduce_scatter | solution.py:314
  928.4 196.2 %reduce-scatter.23.cloned.1.call-start = ((), (), s32[]{:S(2)}) async-start(), calls=%async_computation.23 | async-start | bytes 5898240 | tf_op jit(solution)/shard_map/reduce_scatter | solution.py:302
  951.7 233.4 %reduce-scatter.25.cloned.1.call-start = ((), (), s32[]{:S(2)}) async-start(), calls=%async_computation.24 | async-start | bytes 5898240 | tf_op jit(solution)/shard_map/reduce_scatter | solution.py:305
  960.9 284.3 %reduce-scatter.27.cloned.1.call-start = ((), (), s32[]{:S(2)}) async-start(), calls=%async_computation.25 | async-start | bytes 5898240 | tf_op jit(solution)/shard_map/reduce_scatter | solution.py:308
  996.8 372.2 %reduce-scatter.31.cloned.1.call-start = ((), (), s32[]{:S(2)}) async-start(), calls=%async_computation.27 | async-start | bytes 15728640 | tf_op jit(solution)/shard_map/reduce_scatter | solution.py:320
  1004.6 488.2 %reduce-scatter.33.cloned.1.call-start = ((), (), s32[]{:S(2)}) async-start(), calls=%async_computation.28 | async-start | bytes 15728640 | tf_op jit(solution)/shard_map/reduce_scatter | solution.py:323
  1012.2 604.5 %reduce-scatter.35.cloned.1.call-start = ((), (), s32[]{:S(2)}) async-start(), calls=%async_computation.29 | async-start | bytes 15728640 | tf_op jit(solution)/shard_map/reduce_scatter | solution.py:326
  1020.3 668.4 %reduce-scatter.41.cloned.1.call-start = ((), (), s32[]{:S(2)}) async-start(), calls=%async_computation.33 | async-start | bytes 491520
  1022.3 935.4 %all-reduce.9.cloned.1.call-start = ((), (), s32[]{:S(2)}) async-start(), calls=%async_computation.35 | async-start | bytes 30670848 | tf_op jit(solution)/shard_map/psum | solution.py:332
  (145 other events, 1355.3 us)
Sparse Core Ops, SparseCore 0:
  9.9 60.0 all-gather.18
  71.8 58.0 all-gather.16
  131.7 57.6 all-gather.22
  191.1 57.1 all-gather.14
  250.5 30.9 all-gather.34
  283.8 30.8 all-gather.20
  317.1 30.9 all-gather.24
  349.9 57.0 all-gather.26
  408.9 122.5 all-gather.28
  533.1 122.5 all-gather.30
  657.5 122.5 all-gather.32
  843.6 30.9 reduce-scatter.36
  878.1 30.9 reduce-scatter.38
  912.5 30.9 reduce-scatter.42
  946.9 57.0 reduce-scatter.20
  1006.9 57.0 reduce-scatter.28
  1067.4 57.0 reduce-scatter.22
  1128.0 57.0 reduce-scatter.24
  1188.1 57.0 reduce-scatter.26
  1248.2 120.7 reduce-scatter.30
  1372.0 120.7 reduce-scatter.32
  1495.9 120.7 reduce-scatter.34
  1620.0 24.5 reduce-scatter.40
  1647.4 310.1 all-reduce.8
where the time goes:
time: 2000 us; the launch traced here: 1990 us
  waiting for transfers between devices  1330 us (66%)
  matrix products  278 us (14%)
  other arithmetic  163 us (8%)
  blocking collectives  105 us (5%)
  local copies, waits for them, and re-layouts  78.5 us (4%)
  between operations  24 us (1%)
    psum x1, waiting for transfers between devices, per_device(): lax.psum(part_sums[1].astype(jnp.bfloat16), 'rep').astype(jnp.float32)  238 us
    reduce_scatter x1, waiting for transfers between devices, per_device(): lax.psum_scatter(g_up.astype(jnp.bfloat16), 'shard', scatter_dimension=0,...  124 us
    reduce_scatter x1, waiting for transfers between devices, per_device(): lax.psum_scatter(g_down.astype(jnp.bfloat16), 'shard', scatter_dimension=...  124 us
    reduce_scatter x1, waiting for transfers between devices, per_device(): lax.psum_scatter(g_gate.astype(jnp.bfloat16), 'shard', scatter_dimension=...  124 us
    all_gather x1, waiting for transfers between devices, per_device(): lax.all_gather(w_gate, 'shard', axis=0, tiled=True)  118 us
    another operation x4, other arithmetic, attend(): jax.scipy.linalg.solve_triangular(system, coupled, lower=True, unit_diago...  118 us
    all_gather x1, waiting for transfers between devices, per_device(): lax.all_gather(w_down, 'shard', axis=0, tiled=True)  117 us
    all_gather x1, waiting for transfers between devices, per_device(): lax.all_gather(w_up, 'shard', axis=0, tiled=True)  116 us
  transfers between devices with their start and end apart: 24, of which 16 were waited for; matrix products, arithmetic and copies ran while one was open for 21% of the time, Pallas kernels for 0%

commit v1 on v0

--- a/solution.py
+++ b/solution.py
@@ -5,6 +5,22 @@
 
 eps = 1e-06
 highest = lax.Precision.HIGHEST
+
+
+def collect(x, axis, dim):
+    ways, here, step = (lax.axis_size(axis), lax.axis_index(axis), x.shape[dim])
+    lengths = [n * ways if d == dim else n for d, n in enumerate(x.shape)]
+    full = lax.dynamic_update_slice_in_dim(jnp.zeros(lengths, x.dtype), x, here * step, axis=dim)
+    going_up = going_down = x
+    for far in range(1, ways // 2 + 1):
+        going_up = lax.ppermute(going_up, axis, [(d, (d + 1) % ways) for d in range(ways)])
+        full = lax.dynamic_update_slice_in_dim(full, going_up, (here - far) % ways * step, axis=dim)
+        if 2 * far < ways:
+            going_down = lax.ppermute(going_down, axis, [(d, (d - 1) % ways) for d in range(ways)])
+            full = lax.dynamic_update_slice_in_dim(
+                full, going_down, (here + far) % ways * step, axis=dim
+            )
+    return full
 
 
 def rms_norm(value, gain_vec):
@@ -158,7 +174,7 @@
         lax.all_gather(w_beta, "shard", axis=0, tiled=True),
         lax.all_gather(w_out, "shard", axis=0, tiled=True),
         lax.all_gather(gain_two, "shard", axis=0, tiled=True),
-        lax.all_gather(w_gate, "shard", axis=0, tiled=True),
+        collect(w_gate, "shard", 0),
         lax.all_gather(w_up, "shard", axis=0, tiled=True),
         lax.all_gather(w_down, "shard", axis=0, tiled=True),
     )

time: 2000 us -> 2020 us (1.010)
  blocking collectives: 105 us -> 266 us
  waiting for transfers between devices: 1330 us -> 1170 us
  local copies, waits for them, and re-layouts: 78.5 us -> 111 us
    all_gather x1, blocking collectives: 8.08 us -> 169 us  [per_device(): lax.all_gather(gain_two, 'shard', axis=0, tiled=True)]
    all_gather x1 -> x0, waiting for transfers between devices: 118 us -> none  [per_device(): lax.all_gather(w_gate, 'shard', axis=0, tiled=True)]
    ppermute x0 -> x3, waiting for transfers between devices: none -> 107 us  [the longest x2 107 us: collect(): lax.ppermute(going_up, axis, [(d, (d + 1) % ways) for d in range(ways)])]
    all_gather x1, waiting for transfers between devices: 116 us -> 40.9 us  [per_device(): lax.all_gather(w_up, 'shard', axis=0, tiled=True)]
    reduce_scatter x1, waiting for transfers between devices: 0.02 us -> 60.5 us  [per_device(): lax.psum_scatter(g_query.astype(jnp.bfloat16), 'shard', scatter_dimension...]
    all_gather x1, waiting for transfers between devices: 36 us -> 0.01 us  [per_device(): lax.all_gather(w_out, 'shard', axis=0, tiled=True)]
    reduce_scatter x1, waiting for transfers between devices: 41.7 us -> 6.04 us  [per_device(): lax.psum_scatter(g_out.astype(jnp.bfloat16), 'shard', scatter_dimension=0...]
    all_gather x1, waiting for transfers between devices: 29.7 us -> 0.02 us  [per_device(): lax.all_gather(key_end.astype(jnp.bfloat16), 'shard', axis=0, tiled=True)]
  transfers between devices with their start and end apart: 24 -> 26, of which waited for: 16 -> 13; matrix products, arithmetic and copies ran while one was open for 21% -> 22% of each run, Pallas kernels for 0% -> 0%
where the time goes in v1:
time: 2020 us; the launch traced here: 2010 us
  waiting for transfers between devices  1170 us (58%)
  matrix products  273 us (14%)
  blocking collectives  266 us (13%)
  other arithmetic  161 us (8%)
  local copies, waits for them, and re-layouts  111 us (5%)
  between operations  23.7 us (1%)
    psum x1, waiting for transfers between devices, per_device(): lax.psum(part_sums[1].astype(jnp.bfloat16), 'rep').astype(jnp.float32)  238 us
    all_gather x1, blocking collectives, per_device(): lax.all_gather(gain_two, 'shard', axis=0, tiled=True)  169 us
    reduce_scatter x1, waiting for transfers between devices, per_device(): lax.psum_scatter(g_gate.astype(jnp.bfloat16), 'shard', scatter_dimension=...  124 us
    reduce_scatter x1, waiting for transfers between devices, per_device(): lax.psum_scatter(g_down.astype(jnp.bfloat16), 'shard', scatter_dimension=...  124 us
    reduce_scatter x1, waiting for transfers between devices, per_device(): lax.psum_scatter(g_up.astype(jnp.bfloat16), 'shard', scatter_dimension=0,...  124 us
    another operation x4, other arithmetic, attend(): jax.scipy.linalg.solve_triangular(system, coupled, lower=True, unit_diago...  118 us
    all_gather x1, waiting for transfers between devices, per_device(): lax.all_gather(w_down, 'shard', axis=0, tiled=True)  116 us
    ppermute x2, waiting for transfers between devices, collect(): lax.ppermute(going_up, axis, [(d, (d + 1) % ways) for d in range(ways)])  107 us
  transfers between devices with their start and end apart: 26, of which 13 were waited for; matrix products, arithmetic and copies ran while one was open for 22% of the time, Pallas kernels for 0%

profile of v1, /device:TPU:0, one launch (start us, length us, event | category | flops | bytes accessed | tf_op | source)
XLA Modules:
  0.0 2010.4 jit_solution(3507874786225423820)
XLA Ops:
  10.1 9.5 all-gather.1
  19.6 8.5 all_gather.43
  29.3 40.6 %all-gather.18.cloned.1.call-done = bf16[1536,1536]{1,0:T(8,128)(2,1)} async-done(((bf16[384,1536]{1,0:T(8,128)(2,1)}), bf16[1536,1536]{1,0:T(8,128)(2,1)}) %all-gather.18.cloned.1.call-update) | async-done | bytes 4718608 | tf_op jit(solution)/shard_map/all_gather | solution.py:173
  76.4 117.9 %custom-call.16 = f32[12,1,128,128]{2,3,1,0:T(8,128)S(1)} custom-call(f32[12,1,128,128]{3,2,1,0:T(8,128)S(1)} %add_bitcast_fusion), custom_call_target="InvertDiagBlocksLowerTriangular" | custom-call | tf_op jit(solution)/shard_map/jvp(jit(_solve_triangular))/vmap()/triangular_solve/custom-call.1 | solution.py:105
  216.5 107.2 %collective-permute-done = bf16[384,4096]{1,0:T(8,128)(2,1)} collective-permute-done((bf16[384,4096]{1,0:T(8,128)(2,1)}, bf16[384,4096]{1,0:T(8,128)(2,1)}, u32[]{:S(2)}, u32[]{:S(2)}) %collective-permute-start) | collective-permute-done | bytes 3145760 | tf_op jit(solution)/shard_map/ppermute | solution.py:16
  326.1 168.6 %all-gather.2 = bf16[4,1,384]{2,1,0:T(2,128)(2,1)S(1)} all-gather(bf16[1,1,384]{2,1,0:T(2,128)(2,1)S(1)} %reshape.387), channel_id=1, replica_groups=mesh['rep'=8,'shard'=4] {'shard'}, dimensions={0}, use_global_device_ids=true | all-gather | bytes 3840 | tf_op jit(solution)/shard_map/all_gather | solution.py:176
  547.2 30.1 %while.31 = (s32[]{:T(128)}, f32[12,128,128]{1,2,0:T(8,128)}, f32[4,12,128,128]{2,3,1,0:T(8,128)}, pred[4]{0:T(512)(128)(4,1)}, s32[4]{0:T(128)}, /*index=5*/s32...) while((s32[]{:T(128)}, f32[12,128,128]{1,2,0:T(8,128)}, f32[4,12,128,128]{2,3,1,0:T(8,128)}, ...), condition=%wide.region_4.7_spmd, body=%wide.region_3.6_spmd.sunk | while | flops 302186496 | bytes 6291597 | solution.py:126
  612.1 40.9 %all-gather.28.cloned.1.call-done = bf16[1536,4096]{1,0:T(8,128)(2,1)} async-done(((bf16[384,4096]{1,0:T(8,128)(2,1)}), bf16[1536,4096]{1,0:T(8,128)(2,1)}) %all-gather.28.cloned.1.call-update) | async-done | bytes 12582928 | tf_op jit(solution)/shard_map/all_gather | solution.py:178
  660.8 116.4 %all-gather.30.cloned.1.call-done = bf16[4096,1536]{1,0:T(8,128)(2,1)} async-done(((bf16[1024,1536]{1,0:T(8,128)(2,1)}), bf16[4096,1536]{1,0:T(8,128)(2,1)}) %all-gather.30.cloned.1.call-update) | async-done | bytes 12582928 | tf_op jit(solution)/shard_map/all_gather | solution.py:179
  777.2 10.3 fusion.171
  787.5 10.6 multiply_convert_fusion.1
  804.9 10.4 multiply_reduce_fusion
  857.4 42.1 %while.32 = (s32[]{:T(128)}, f32[12,128,128]{2,1,0:T(8,128)}, bf16[4,12,128,128]{3,2,1,0:T(8,128)(2,1)}, f32[4,12,128,128]{3,2,1,0:T(8,128)}, pred[4]{0:T(512)(1...) while((s32[]{:T(128)}, f32[12,128,128]{2,1,0:T(8,128)}, ...), condition=%wide.region_16.19_spmd.clone, body=%wide.region_15.18_spmd.clone.sunk | while | flops 605552640 | bytes 7869037 | solution.py:126
  1025.0 60.5 %reduce-scatter.21.cloned.1.call-done = bf16[384,1536]{1,0:T(8,128)(2,1)} async-done(((bf16[1536,1536]{1,0:T(8,128)(2,1)}), bf16[384,1536]{1,0:T(8,128)(2,1)}) %reduce-scatter.21.cloned.1.call-update) | async-done | bytes 1179664 | tf_op jit(solution)/shard_map/reduce_scatter | solution.py:315
  1085.5 60.0 %reduce-scatter.27.cloned.1.call-done = bf16[384,1536]{1,0:T(8,128)(2,1)} async-done(((bf16[1536,1536]{1,0:T(8,128)(2,1)}), bf16[384,1536]{1,0:T(8,128)(2,1)}) %reduce-scatter.27.cloned.1.call-update) | async-done | bytes 1179664 | tf_op jit(solution)/shard_map/reduce_scatter | solution.py:324
  1145.5 60.5 %reduce-scatter.25.cloned.1.call-done = bf16[384,1536]{1,0:T(8,128)(2,1)} async-done(((bf16[1536,1536]{1,0:T(8,128)(2,1)}), bf16[384,1536]{1,0:T(8,128)(2,1)}) %reduce-scatter.25.cloned.1.call-update) | async-done | bytes 1179664 | tf_op jit(solution)/shard_map/reduce_scatter | solution.py:321
  1206.1 60.6 %reduce-scatter.23.cloned.1.call-done = bf16[384,1536]{1,0:T(8,128)(2,1)} async-done(((bf16[1536,1536]{1,0:T(8,128)(2,1)}), bf16[384,1536]{1,0:T(8,128)(2,1)}) %reduce-scatter.23.cloned.1.call-update) | async-done | bytes 1179664 | tf_op jit(solution)/shard_map/reduce_scatter | solution.py:318
  1266.6 123.9 %reduce-scatter.31.cloned.1.call-done = bf16[384,4096]{1,0:T(8,128)(2,1)} async-done(((bf16[1536,4096]{1,0:T(8,128)(2,1)}), bf16[384,4096]{1,0:T(8,128)(2,1)}) %reduce-scatter.31.cloned.1.call-update) | async-done | bytes 3145744 | tf_op jit(solution)/shard_map/reduce_scatter | solution.py:336
  1390.5 123.7 %reduce-scatter.33.cloned.1.call-done = bf16[384,4096]{1,0:T(8,128)(2,1)} async-done(((bf16[1536,4096]{1,0:T(8,128)(2,1)}), bf16[384,4096]{1,0:T(8,128)(2,1)}) %reduce-scatter.33.cloned.1.call-update) | async-done | bytes 3145744 | tf_op jit(solution)/shard_map/reduce_scatter | solution.py:339
  1514.2 123.9 %reduce-scatter.35.cloned.1.call-done = bf16[1024,1536]{1,0:T(8,128)(2,1)} async-done(((bf16[4096,1536]{1,0:T(8,128)(2,1)}), bf16[1024,1536]{1,0:T(8,128)(2,1)}) %reduce-scatter.35.cloned.1.call-update) | async-done | bytes 3145744 | tf_op jit(solution)/shard_map/reduce_scatter | solution.py:342
  1655.1 40.3 %all-reduce.3 = (f32[]{:T(128)}, f32[]{:T(128)}, f32[]{:T(128)}, f32[]{:T(128)}) all-reduce(f32[]{:T(128)} %get-tuple-element.278, f32[]{:T(128)} %get-tuple-element.326, f32[]{:T(128)} %get-tuple-element.280, f32[]{:T(128)} %get-tuple-element.279), channel_id=1, replica_groups=mesh['rep'=8,'shard'=4] {'rep','shard'}, use_global_device_ids=true, to_apply=%region_52.55 | all-reduce | flops 4 | bytes 32 | tf_op jit(solution)/shard_map/psum | solution.py:359
  1698.2 10.8 all-reduce.6
  1711.2 28.2 %all-reduce.4 = (bf16[384]{0:T(512)(128)(2,1)S(1)}, bf16[384,12]{0,1:T(8,128)(2,1)S(1)}, bf16[384]{0:T(512)(128)(2,1)S(1)}) all-reduce(bf16[384]{0:T(512)(128)(2,1)S(1)} %dynamic-slice.3, bf16[384,12]{0,1:T(8,128)(2,1)S(1)} %copy.335, bf16[384]{0:T(512)(128)(2,1)S(1)} %dynamic-slice.5), channel_id=1, replica_groups=mesh['rep'=8,'shard'=4] {'rep'}, use_global_device_ids=true, to_apply=%region_29.32 | all-reduce | flops 5376 | bytes 21504 | tf_op jit(solution)/shard_map/psum | solution.py:347
  1741.1 238.1 %all-reduce.9.cloned.1.call-done = (bf16[384,1536]{1,0:T(8,128)(2,1)}, bf16[384,1536]{1,0:T(8,128)(2,1)}, bf16[384,1536]{1,0:T(8,128)(2,1)}, bf16[384,1536]{1,0:...) async-done(((bf16[384,1536]{1,0:T(8,128)(2,1)}, bf16[384,1536]{1,0:T(8,128)(2,1)}, ...) | async-done | bytes 15335440 | tf_op jit(solution)/shard_map/psum | solution.py:348
  (580 shorter events, 412.6 us)
Async XLA Ops:
  7.9 191.5 %all-gather.16.cloned.1.call-start = ((), (), s32[]{:S(2)}) async-start(), calls=%async_computation.13 | async-start | bytes 5898240 | tf_op jit(solution)/shard_map/all_gather | solution.py:171
  8.7 198.7 %all-gather.22.cloned.1.call-start = ((), (), s32[]{:S(2)}) async-start(), calls=%async_computation.16 | async-start | bytes 5898240 | tf_op jit(solution)/shard_map/all_gather | solution.py:172
  9.4 509.6 %all-gather.14.cloned.1.call-start = ((), (), s32[]{:S(2)}) async-start(), calls=%async_computation.12 | async-start | bytes 5898240 | tf_op jit(solution)/shard_map/all_gather | solution.py:170
  10.0 524.1 %all-gather.32.cloned.1.call-start = ((), (), s32[]{:S(2)}) async-start(), calls=%async_computation.29 | async-start | bytes 1966080 | tf_op jit(solution)/shard_map/all_gather | solution.py:207
  199.0 336.8 %all-gather.20.cloned.1.call-start = ((), (), s32[]{:S(2)}) async-start(), calls=%async_computation.15 | async-start | bytes 1966080 | tf_op jit(solution)/shard_map/all_gather | solution.py:201
  207.4 380.8 %all-gather.24.cloned.1.call-start = ((), (), s32[]{:S(2)}) async-start(), calls=%async_computation.17 | async-start | bytes 1966080 | tf_op jit(solution)/shard_map/all_gather | solution.py:204
  211.4 394.5 %all-gather.26.cloned.1.call-start = ((), (), s32[]{:S(2)}) async-start(), calls=%async_computation.18 | async-start | bytes 5898240 | tf_op jit(solution)/shard_map/all_gather | solution.py:175
  212.1 440.8 %all-gather.28.cloned.1.call-start = ((), (), s32[]{:S(2)}) async-start(), calls=%async_computation.19 | async-start | bytes 15728640 | tf_op jit(solution)/shard_map/all_gather | solution.py:178
  212.9 564.3 %all-gather.30.cloned.1.call-start = ((), (), s32[]{:S(2)}) async-start(), calls=%async_computation.20 | async-start | bytes 15728640 | tf_op jit(solution)/shard_map/all_gather | solution.py:179
  213.5 731.2 %reduce-scatter.37.cloned.1.call-start = ((), (), s32[]{:S(2)}) async-start(), calls=%async_computation.30 | async-start | bytes 1966080
  213.5 110.2 %collective-permute-start = (bf16[384,4096]{1,0:T(8,128)(2,1)}, bf16[384,4096]{1,0:T(8,128)(2,1)}, u32[]{:S(2)}, u32[]{:S(2)}) collective-permute-start(bf16[384,4096]{1,0:T(8,128)(2,1)} %param.33), channel_id=1, source_target_pairs={{0,1},{1,2},{2,3},{3,0},{4,5},{5,6},{6,7},{7,4},{8,9},{9,10},{10,1... | collective-permute-start | bytes 9437192 | tf_op jit(solution)/shard_map/ppermute | solution.py:16
  215.1 295.1 %collective-permute-start.1 = (bf16[384,4096]{1,0:T(8,128)(2,1)}, bf16[384,4096]{1,0:T(8,128)(2,1)}, u32[]{:S(2)}, u32[]{:S(2)}) collective-permute-start(bf16[384,4096]{1,0:T(8,128)(2,1)} %param.33), channel_id=1, source_target_pairs={{0,3},{1,0},{2,1},{3,2},{4,7},{5,4},{6,5},{7,6},{8,11},{9,8},{10,9... | collective-permute-start | bytes 9437192 | tf_op jit(solution)/shard_map/ppermute | solution.py:19
  323.7 190.4 %collective-permute-start.2 = (bf16[384,4096]{1,0:T(8,128)(2,1)}, bf16[384,4096]{1,0:T(8,128)(2,1)}, u32[]{:S(2)}, u32[]{:S(2)}) collective-permute-start(bf16[384,4096]{1,0:T(8,128)(2,1)} %collective-permute-done), channel_id=1, source_target_pairs={{0,1},{1,2},{2,3},{3,0},{4,5},{5,6},{6,7},{7,4},{8,9},{9,10},{10,1... | collective-permute-start | bytes 9437192 | tf_op jit(solution)/shard_map/ppermute | solution.py:16
  849.0 101.3 %reduce-scatter.43.cloned.1.call-start = ((), (), s32[]{:S(2)}) async-start(), calls=%async_computation.33 | async-start | bytes 1966080
  908.4 116.6 %reduce-scatter.29.cloned.1.call-start = ((), (), s32[]{:S(2)}) async-start(), calls=%async_computation.25 | async-start | bytes 5898240 | tf_op jit(solution)/shard_map/reduce_scatter | solution.py:330
  913.1 172.4 %reduce-scatter.21.cloned.1.call-start = ((), (), s32[]{:S(2)}) async-start(), calls=%async_computation.21 | async-start | bytes 5898240 | tf_op jit(solution)/shard_map/reduce_scatter | solution.py:315
  929.6 215.9 %reduce-scatter.27.cloned.1.call-start = ((), (), s32[]{:S(2)}) async-start(), calls=%async_computation.24 | async-start | bytes 5898240 | tf_op jit(solution)/shard_map/reduce_scatter | solution.py:324
  978.9 227.2 %reduce-scatter.25.cloned.1.call-start = ((), (), s32[]{:S(2)}) async-start(), calls=%async_computation.23 | async-start | bytes 5898240 | tf_op jit(solution)/shard_map/reduce_scatter | solution.py:321
  985.6 281.0 %reduce-scatter.23.cloned.1.call-start = ((), (), s32[]{:S(2)}) async-start(), calls=%async_computation.22 | async-start | bytes 5898240 | tf_op jit(solution)/shard_map/reduce_scatter | solution.py:318
  993.2 397.3 %reduce-scatter.31.cloned.1.call-start = ((), (), s32[]{:S(2)}) async-start(), calls=%async_computation.26 | async-start | bytes 15728640 | tf_op jit(solution)/shard_map/reduce_scatter | solution.py:336
  1001.1 513.1 %reduce-scatter.33.cloned.1.call-start = ((), (), s32[]{:S(2)}) async-start(), calls=%async_computation.27 | async-start | bytes 15728640 | tf_op jit(solution)/shard_map/reduce_scatter | solution.py:339
  1008.8 629.3 %reduce-scatter.35.cloned.1.call-start = ((), (), s32[]{:S(2)}) async-start(), calls=%async_computation.28 | async-start | bytes 15728640 | tf_op jit(solution)/shard_map/reduce_scatter | solution.py:342
  1017.0 693.3 %reduce-scatter.41.cloned.1.call-start = ((), (), s32[]{:S(2)}) async-start(), calls=%async_computation.32 | async-start | bytes 491520
  1018.9 960.3 %all-reduce.9.cloned.1.call-start = ((), (), s32[]{:S(2)}) async-start(), calls=%async_computation.34 | async-start | bytes 30670848 | tf_op jit(solution)/shard_map/psum | solution.py:348
  (156 other events, 2496.7 us)
Sparse Core Ops, SparseCore 0:
  9.9 60.0 all-gather.17
  71.8 58.0 all-gather.15
  131.7 57.6 all-gather.21
  191.1 83.4 all-gather.13
  276.8 43.6 all-gather.31
  322.8 93.5 all-gather.19
  418.8 43.7 all-gather.23
  464.4 64.1 all-gather.25
  530.4 122.5 all-gather.27
  654.7 122.5 all-gather.29
  849.1 30.8 reduce-scatter.36
  899.6 30.9 reduce-scatter.42
  934.1 30.8 reduce-scatter.38
  967.9 57.0 reduce-scatter.28
  1028.4 57.0 reduce-scatter.20
  1088.4 57.0 reduce-scatter.26
  1148.9 57.0 reduce-scatter.24
  1209.5 57.0 reduce-scatter.22
  1269.7 120.7 reduce-scatter.30
  1393.5 120.7 reduce-scatter.32
  1517.3 120.7 reduce-scatter.34
  1641.4 24.5 reduce-scatter.40
  1669.0 310.1 all-reduce.8
